TPU v7x, 256 devices: a whole 4x4x8 slice. The times are simulated.
256 devices in a mesh: batch: 8 (over z), queue: 32 (over x, y, core).
Axes of the slice: x: 4, y: 4, z: 8, core: 2. Of those that a mesh axis runs over, the one named last changes fastest.
Arguments:
- key_inputs: bfloat16 [8192, 1024], P('batch'), may hold values from -6 to 6
- head_in: bfloat16 [4096, 1024], P('queue'), may hold values from -0.1875 to 0.1875
- head_out: bfloat16 [4096, 1024], P('queue'), may hold values from -0.09375 to 0.09375
- queue_keys: bfloat16 [131072, 1024], P('queue'), may hold values from -1 to 1
- slots: int32 [8192], replicated, may hold values from 0 to 131071, as said below
- questions: bfloat16 [4096, 1024], P(('batch', 'queue')), may hold values from -4 to 4
- positives: int32 [4096], P('batch'), may hold values from 0 to 131071
Outputs:
- queue_out: bfloat16 [131072, 1024], P('queue')
- loss: float32 [], replicated
- question_grads: float32 [4096, 1024], P(('batch', 'queue'))
Inputs may be any that keep to these rules, and one draw needn't show every extreme that they name: The 8192 slots are distinct. In each aligned block of 32 rows, exactly 1 row name slots in each range o * 4096 to o * 4096 + 4095.
All inputs are finite; a program needn't handle non-finite values.
Results may differ from a plain program's by a relative error of at most 0.0025.
Values may be sent and summed in bfloat16 or wider, within the bound.
A program may use at most 128 MiB of HBM per device.

v0:
```python
import jax
import jax.numpy as jnp
from jax import lax
from jax.sharding import PartitionSpec as P

inverse_temp = 20.0
epsilon = 1e-06


def first_layer(key_rows, weight_rows):
    return jax.nn.gelu(
        lax.dot_general(
            key_rows, weight_rows, (((1,), (1,)), ((), ())), preferred_element_type=jnp.float32
        )
    ).astype(jnp.bfloat16)


def body(key_inputs, head_in, head_out, queue_keys, slots, questions, positives):
    seg_len = queue_keys.shape[0]
    feature_dim = queue_keys.shape[1]
    owner_count = lax.axis_size("queue")
    own_index = lax.axis_index("queue")
    batch_rows = key_inputs.shape[0]
    dev_rows = batch_rows // owner_count
    owner_rows = dev_rows // owner_count
    batch_slots = lax.dynamic_slice_in_dim(slots, lax.axis_index("batch") * batch_rows, batch_rows)
    slot_owner = batch_slots // seg_len
    hidden = first_layer(key_inputs, head_in)
    summed = lax.psum_scatter(
        jnp.dot(hidden, head_out, preferred_element_type=jnp.float32),
        "queue",
        scatter_dimension=0,
        tiled=True,
    )
    inverse_norm = lax.rsqrt(jnp.sum(summed * summed, axis=1, keepdims=True) + epsilon)
    encoded = (summed * inverse_norm).astype(jnp.bfloat16)
    own_owner = lax.dynamic_slice_in_dim(slot_owner, own_index * dev_rows, dev_rows)
    ranking = jnp.argsort(own_owner, stable=True)
    packed = encoded[ranking].reshape(owner_count, owner_rows, feature_dim)
    arrived = lax.all_to_all(packed, "queue", split_axis=0, concat_axis=0, tiled=True).reshape(
        dev_rows, feature_dim
    )
    incoming = lax.all_gather(arrived, "batch", axis=0, tiled=True)
    hit_rows = jnp.nonzero(slots // seg_len == own_index, size=incoming.shape[0])[0]
    offsets = slots[hit_rows] - own_index * seg_len
    queue_out = queue_keys.at[offsets].set(incoming)
    logits = inverse_temp * lax.dot_general(
        lax.all_gather(questions, "queue", axis=0, tiled=True),
        queue_out,
        (((1,), (1,)), ((), ())),
        preferred_element_type=jnp.float32,
    )
    local_pos = positives - own_index * seg_len
    inside = (local_pos >= 0) & (local_pos < seg_len)
    clipped = jnp.clip(local_pos, 0, seg_len - 1)
    picked = jnp.take_along_axis(logits, clipped[:, None], axis=1)[:, 0]
    pos_part = jnp.where(inside, picked, jnp.zeros_like(picked))
    local_top = jnp.max(logits, axis=1)
    row_top = lax.pmax(local_top, "queue")
    row_total, pos_logit = lax.psum(
        (jnp.sum(jnp.exp(logits - row_top[:, None]), axis=1), pos_part), "queue"
    )
    log_total = row_top + jnp.log(row_total)
    weights = jnp.exp(logits - log_total[:, None]).astype(jnp.bfloat16)
    product = jnp.dot(weights, queue_out, preferred_element_type=jnp.float32)
    positive_rows = queue_out[clipped].astype(jnp.float32)
    question_grads = lax.psum_scatter(
        inverse_temp
        * (product - jnp.where(inside[:, None], positive_rows, jnp.zeros_like(positive_rows))),
        "queue",
        scatter_dimension=0,
        tiled=True,
    )
    local_loss = jnp.sum(log_total - pos_logit)
    loss = lax.psum(local_loss, "batch") / (logits.shape[0] * lax.axis_size("batch"))
    return (queue_out, loss, question_grads)


def solution(mesh):
    placed = (
        P("batch", None),
        P("queue", None),
        P("queue", None),
        P("queue", None),
        P(),
        P(("batch", "queue"), None),
        P("batch"),
    )
    return jax.shard_map(
        body,
        mesh=mesh,
        in_specs=placed,
        out_specs=(P("queue", None), P(), P(("batch", "queue"), None)),
        check_vma=False,
    )
```

profile of v0, /device:TPU:1, one launch (start us, length us, event | category | flops | bytes accessed | tf_op | source)
XLA Modules:
  0.0 439.8 jit_solution(16589782563543364862)
XLA Ops:
  7.2 0.0 copy-start
  7.2 0.0 copy-start.3
  7.2 0.0 copy-start.4
  7.2 0.0 reduce-scatter.3.cloned.1.call-start
  7.2 7.9 %copy.16 = bf16[4096,1024]{1,0:T(8,128)(2,1)} copy(bf16[4096,1024]{1,0:T(8,128)(2,1)} %param.10) | data formatting | bytes 16777216
  15.2 0.0 copy-done
  15.2 0.0 copy-done.3
  15.2 0.0 copy-done.4
  15.2 0.0 copy-start.1
  15.2 0.0 copy-start.5
  15.2 4.1 fusion.12
  19.3 0.0 reduce-scatter.3.cloned.1.call-update
  19.3 0.0 all-gather.3.cloned.1.call-start
  19.4 0.7 all-gather.3.cloned.1.call-update
  20.1 0.0 copy-done.1
  20.1 0.7 convert_reduce_fusion
  20.8 0.3 reduce-window.16
  21.0 0.1 slice.26
  21.1 0.1 reduce-window.19
  21.2 0.1 slice_reduce_fusion
  21.3 0.1 broadcast_add_fusion
  21.5 57.0 %scatter_custom_fusion = s32[256]{0:T(256)S(1)} fusion(s32[8192]{0:T(1024)S(1)} %bitcast.33, s32[8192]{0:T(1024)S(1)} %ne.62, s32[]{:T(128)} %constant.57.clone.1), kind=kCustom, calls=%fused_computation.77 | custom fusion | flops 8192 | bytes 1028 | tf_op jit(solution)/shard_map/scatter-add | solution.py:44
  78.5 0.3 reduce-window.24
  78.8 0.1 slice.16
  78.9 0.1 slice_reduce_fusion.1
  79.0 0.1 broadcast_add_fusion.1
  79.1 0.7 compare_select_fusion.2
  79.8 1.7 gather_fusion
  81.5 0.1 dynamic_slice.7
  81.6 1.6 sort.17
  83.2 0.0 copy-done.5
  83.3 27.8 %reduce-scatter.3.cloned.1.call-done = f32[32,1024]{1,0:T(8,128)} async-done(((f32[1024,1024]{1,0:T(8,128)}), f32[32,1024]{1,0:T(8,128)}) %reduce-scatter.3.cloned.1.call-update) | async-done | bytes 131088 | tf_op jit(solution)/shard_map/reduce_scatter | solution.py:29
  111.1 1.0 multiply_reduce_fusion.1
  112.2 1.0 multiply_convert_fusion
  113.2 0.6 gather_fusion.1
  113.8 0.5 broadcast.233
  114.3 0.7 reduce.5
  115.0 0.7 reshape.250
  115.6 7.3 %all-to-all-start = ((bf16[32,2,512]{2,1,0:T(2,128)(2,1)}), bf16[32,2,512]{2,1,0:T(2,128)(2,1)S(1)}, u32[]{:S(2)}, u32[]{:S(2)}) async-start(bf16[32,2,512]{2,1,0:T(2,128)(2,1)} %reshape.250), calls=%async_computation.1 | async-start | bytes 131072 | tf_op jit(solution)/shard_map/all_to_all | solution.py:40
  122.9 0.0 reduce-scatter.5.cloned.1.call-start
  123.0 7.3 %all-to-all-done = bf16[32,2,512]{2,1,0:T(2,128)(2,1)S(1)} async-done(((bf16[32,2,512]{2,1,0:T(2,128)(2,1)}), bf16[32,2,512]{2,1,0:T(2,128)(2,1)S(1)}, u32[]{:S(2)}, u32[]{:S(2)}) %all-to-all-start) | async-done | bytes 65568 | tf_op jit(solution)/shard_map/all_to_all | solution.py:40
  130.3 0.1 reshape.251
  130.4 21.3 %all-gather = bf16[256,1,1024]{2,0,1:T(8,128)(2,1)S(1)} all-gather(bf16[32,1,1024]{2,0,1:T(8,128)(2,1)S(1)} %copy.12), channel_id=2, replica_groups=mesh['batch'=8,'queue'=32] {'batch'}, dimensions={0}, use_global_device_ids=true | all-gather | bytes 589824 | tf_op jit(solution)/shard_map/all_gather | solution.py:43
  151.7 10.2 %scatter_custom_fusion.1 = bf16[4096,1024]{1,0:T(8,128)(2,1)} fusion(bf16[4096,1024]{1,0:T(8,128)(2,1)} %copy.16, s32[256]{0:T(256)S(1)} %bitcast.38, bf16[256,1,1024]{2,0,1:T(8,128)(2,1)S(1)} %all-gather), kind=kCustom, calls=%fused_computation.22 | custom fusion | bytes 8912896 | tf_op jit(solution)/shard_map/scatter | solution.py:46
  161.9 1.5 all-gather.3.cloned.1.call-done
  163.3 7.4 %fusion.36 = f32[4096,512]{1,0:T(8,128)S(1)} fusion(bf16[4096,1024]{1,0:T(8,128)(2,1)} %scatter_custom_fusion.1, bf16[512,1024]{1,0:T(8,128)(2,1)} %all-gather.3.cloned.1.call-done), kind=kOutput, calls=%fused_computation.84 | convolution fusion | flops 4294967296 | bytes 17825792 | tf_op jit(solution)/shard_map/dot_general | solution.py:47
  170.7 0.0 copy-start.2
  170.7 4.6 %multiply_bitcast_fusion = (f32[512,4096]{0,1:T(8,128)}, f32[512]{0:T(512)S(1)}) fusion(f32[4096,512]{1,0:T(8,128)S(1)} %fusion.36), kind=kLoop, calls=%fused_computation.8 | loop fusion | flops 4193792 | bytes 16779264 | tf_op jit(solution)/shard_map/mul | solution.py:47
  175.3 1.2 copy-done.2
  176.4 66.4 %pmax.7 = f32[512]{0:T(512)S(1)} all-reduce(f32[512]{0:T(512)S(1)} %get-tuple-element.14), channel_id=1, replica_groups=mesh['batch'=8,'queue'=32] {'queue'}, use_global_device_ids=true, to_apply=%region_11.12 | all-reduce | flops 512 | bytes 4096 | tf_op jit(solution)/shard_map/pmax | solution.py:59
  242.8 4.8 %exponential_reduce_fusion = f32[512]{0:T(512)S(1)} fusion(f32[512]{0:T(512)S(1)} %pmax.7, f32[4096,512]{1,0:T(8,128)} %copy-done.2), kind=kLoop, calls=%fused_computation.7 | loop fusion | flops 6290944 | bytes 8392704 | tf_op jit(solution)/shard_map/reduce_sum | solution.py:61
  247.7 22.1 %gather_fusion.3 = f32[512]{0:T(512)S(1)} fusion(f32[512,4096]{0,1:T(8,128)} %get-tuple-element.13, s32[512]{0:T(512)S(1)} %bitcast.30), kind=kCustom, calls=%fused_computation.3 | custom fusion | bytes 8192 | tf_op jit(solution)/shard_map/jit(take_along_axis)/gather | solution.py:56
  269.8 7.2 %gather_fusion.2 = bf16[512,1024]{1,0:T(8,128)(2,1)S(1)} fusion(bf16[4096,1024]{1,0:T(8,128)(2,1)} %scatter_custom_fusion.1, s32[1024]{0:T(1024)S(1)} %pad_clamp_fusion), kind=kCustom, calls=%fused_computation.2 | custom fusion | bytes 2099200 | tf_op jit(solution)/shard_map/gather | solution.py:66
  277.0 63.0 %all-reduce = (f32[512]{0:T(512)S(1)}, f32[512]{0:T(512)S(1)}) all-reduce(f32[512]{0:T(512)S(1)} %exponential_reduce_fusion, f32[512]{0:T(512)S(1)} %get-tuple-element.9), channel_id=1, replica_groups=mesh['batch'=8,'queue'=32] {'queue'}, use_global_device_ids=true, to_apply=%region_13.14 | all-reduce | flops 1024 | bytes 8192 | tf_op jit(solution)/shard_map/psum | solution.py:60
  340.0 0.6 subtract_reduce_fusion
  340.6 11.7 %subtract_multiply_fusion = f32[512,1024]{1,0:T(8,128)} fusion(bf16[512,1024]{1,0:T(8,128)(2,1)S(1)} %gather_fusion.2, bf16[4096,1024]{1,0:T(8,128)(2,1)} %scatter_custom_fusion.1, f32[512]{0:T(512)S(1)} %get-tuple-element.8, pred[512]{0:T(512)(128)(4,1)S(1)} %get-tuple-element.10, f32[4096,512]{1,0:T(8,128)} %copy-done.2), kind=kOutput, calls=%fused_computation.12 | convolution fusion | flops 4303355904 | bytes 19925504 | tf_op jit(solution)/shard_map/dot_general | solution.py:65
  352.3 0.0 reduce-scatter.5.cloned.1.call-update
  352.4 12.7 %psum.23 = f32[]{:T(128)} all-reduce(f32[]{:T(128)} %get-tuple-element.7), channel_id=1, replica_groups=mesh['batch'=8,'queue'=32] {'batch'}, use_global_device_ids=true, to_apply=%region_16.17 | all-reduce | flops 1 | bytes 8 | tf_op jit(solution)/shard_map/psum | solution.py:75
  365.7 66.4 %reduce-scatter.5.cloned.1.call-done = f32[16,1024]{1,0:T(8,128)} async-done(((f32[512,1024]{1,0:T(8,128)}), f32[16,1024]{1,0:T(8,128)}) %reduce-scatter.5.cloned.1.call-update) | async-done | bytes 65552 | tf_op jit(solution)/shard_map/reduce_scatter | solution.py:67
  (19 shorter events, 0.2 us)
Async XLA Ops:
  7.2 8.0 %copy-start = (bf16[1024,1024]{1,0:T(8,128)(2,1)S(1)}, bf16[1024,1024]{1,0:T(8,128)(2,1)}, u32[]{:S(2)}) copy-start(bf16[1024,1024]{1,0:T(8,128)(2,1)} %param.7) | copy-start | bytes 6291460
  7.2 8.0 %copy-start.3 = (bf16[128,1024]{1,0:T(8,128)(2,1)S(1)}, bf16[128,1024]{1,0:T(8,128)(2,1)}, u32[]{:S(2)}) copy-start(bf16[128,1024]{1,0:T(8,128)(2,1)} %param.9) | copy-start | bytes 786436
  7.2 8.0 %copy-start.4 = (bf16[128,1024]{1,0:T(8,128)(2,1)S(1)}, bf16[128,1024]{1,0:T(8,128)(2,1)}, u32[]{:S(2)}) copy-start(bf16[128,1024]{1,0:T(8,128)(2,1)} %param.8) | copy-start | bytes 786436
  7.2 103.9 %reduce-scatter.3.cloned.1.call-start = ((), (), s32[]{:S(2)}) async-start(), calls=%async_computation.3 | async-start | bytes 4325376 | tf_op jit(solution)/shard_map/reduce_scatter | solution.py:29
  15.2 4.9 %copy-start.1 = (s32[8192]{0:T(1024)S(1)}, s32[8192]{0:T(1024)}, u32[]{:S(2)}) copy-start(s32[8192]{0:T(1024)} %param.11) | copy-start | bytes 98308
  15.2 68.1 %copy-start.5 = (s32[512]{0:T(512)S(1)}, s32[512]{0:T(512)}, u32[]{:S(2)}) copy-start(s32[512]{0:T(512)} %param.13) | copy-start | bytes 6148
  19.3 144.0 %all-gather.3.cloned.1.call-start = ((), (), s32[]{:S(2)}) async-start(), calls=%async_computation.4 | async-start | bytes 1081344 | tf_op jit(solution)/shard_map/all_gather | solution.py:48
  115.6 14.7 %all-to-all-start = ((bf16[32,2,512]{2,1,0:T(2,128)(2,1)}), bf16[32,2,512]{2,1,0:T(2,128)(2,1)S(1)}, u32[]{:S(2)}, u32[]{:S(2)}) async-start(bf16[32,2,512]{2,1,0:T(2,128)(2,1)} %reshape.250), calls=%async_computation.1 | async-start | bytes 131072 | tf_op jit(solution)/shard_map/all_to_all | solution.py:40
  122.9 309.2 %reduce-scatter.5.cloned.1.call-start = ((), (), s32[]{:S(2)}) async-start(), calls=%async_computation.5 | async-start | bytes 2162688 | tf_op jit(solution)/shard_map/reduce_scatter | solution.py:67
  170.7 5.7 %copy-start.2 = (f32[4096,512]{1,0:T(8,128)}, f32[4096,512]{1,0:T(8,128)S(1)}, u32[]{:S(2)}) copy-start(f32[4096,512]{1,0:T(8,128)S(1)} %fusion.36) | copy-start | bytes 25165828
Sparse Core Ops, SparseCore 0:
  19.4 91.6 reduce-scatter.2
  114.0 49.2 all-gather.2
  352.5 79.5 reduce-scatter.4
where the time goes:
time: 441 us; the launch traced here: 440 us
  blocking collectives  163 us (37%)
  waiting for transfers between devices  104 us (24%)
  other arithmetic  73.6 us (17%)
  local copies, waits for them, and re-layouts  52.7 us (12%)
  matrix products  23.2 us (5%)
  between operations  15.8 us (4%)
  starting transfers between devices  7.42 us (2%)
    pmax x1, blocking collectives, body(): row_top = lax.pmax(local_top, 'queue')  66.4 us
    reduce_scatter x1, waiting for transfers between devices, body(): lax.psum_scatter(inverse_temp * (product - jnp.where(inside[:, None], pos...  66.4 us
    psum x1, blocking collectives, body(): lax.psum((jnp.sum(jnp.exp(logits - row_top[:, None]), axis=1), pos_part),...  63 us
    scatter-add x1, other arithmetic, body(): jnp.nonzero(slots // seg_len == own_index, size=incoming.shape[0])[0]  57 us
    reduce_scatter x1, waiting for transfers between devices, body(): lax.psum_scatter(jnp.dot(hidden, head_out, preferred_element_type=jnp.flo...  27.8 us
    gather x1, local copies, waits for them, and re-layouts, body(): picked = jnp.take_along_axis(logits, clipped[:, None], axis=1)[:, 0]  22.1 us
    all_gather x1, blocking collectives, body(): incoming = lax.all_gather(arrived, 'batch', axis=0, tiled=True)  21.3 us
    psum x1, blocking collectives, body(): lax.psum(local_loss, 'batch') / (logits.shape[0] * lax.axis_size('batch'))  12.7 us
  transfers between devices with their start and end apart: 4, of which 4 were waited for; matrix products, arithmetic and copies ran while one was open for 18% of the time, Pallas kernels for 0%

commit v1 on v0

v1 whole, which is shorter than its diff:
```python
import functools
import math

import jax
import jax.numpy as jnp
from jax import lax
from jax.experimental import pallas as pl
from jax.experimental.pallas import tpu as pltpu
from jax.sharding import PartitionSpec as P

inverse_temp = 20.0
epsilon = 1e-06
log2e = math.log2(math.e)
F32 = jnp.float32
BF16 = jnp.bfloat16
NEG = -1e30
CORES = 2
HALVES = 2


def nt_dot(a, b):
    return lax.dot_general(a, b, (((1,), (1,)), ((), ())), preferred_element_type=F32)


def dot(a, b):
    return jnp.dot(a, b, preferred_element_type=F32)


def iota(shape, axis):
    return lax.broadcasted_iota(jnp.int32, shape, axis)


def rcopy(src, dst, send, recv, device):
    return pltpu.make_async_remote_copy(
        src_ref=src,
        dst_ref=dst,
        send_sem=send,
        recv_sem=recv,
        device_id=device,
        device_id_type=pl.DeviceIdType.MESH,
    )


def peers(count, me, step):
    def one(d, carry):
        step(lax.rem(me + d, count))
        return carry

    lax.fori_loop(1, count, one, 0)


def row_to_col(row, eye):
    return jnp.sum(jnp.where(eye, row, 0.0), axis=1, keepdims=True)


def col_to_row(col, eye):
    return jnp.sum(jnp.where(eye, col, 0.0), axis=0, keepdims=True)


def kernel(
    nb, nq,
    x_hbm, win_hbm, wout_hbm, k_hbm, slots_hbm, q_hbm, pos_hbm,
    k_ref, loss_ref, grads_ref,
    slots_v, pos_v, x_v, win_v, wout_v, part_v, precv_v, q_v, nk_v, s_v, acc_v, pp_v,
    mx_v, slot_v, offrow_v, lp_v, sc_v, stats_v, psend_v, pairr_v, gsend_v, grecv_v, l1_v, l2_v,
    ld_sem, k_sem, w_send, w_recv, q_send, q_recv, qp_sem, p_send, p_recv, z_send, z_recv,
    st_send, st_recv, gp_sem, g_send, g_recv, l1_send, l1_recv, l2_send, l2_recv,
):
    z = lax.axis_index("batch")
    me = lax.axis_index("queue")
    chips = nq // CORES
    chip = me // CORES
    core = lax.rem(me, CORES)
    mate = (z, me + 1 - 2 * core)
    dim = x_v.shape[1]
    rows = x_v.shape[0]
    hid = win_hbm.shape[0]
    seg = k_ref.shape[0]
    nch, _, _, width = s_v.shape
    blocks = rows // nq
    sub = blocks // HALVES
    qrows = q_hbm.shape[0]
    half_q = chips * qrows
    ques = nq * qrows
    fresh = nb * blocks
    lanes = 128
    scale2 = inverse_temp * log2e

    def same_core(j):
        return (z, j * CORES + core)

    barrier = pltpu.get_barrier_semaphore()

    def greet(device):
        pl.semaphore_signal(barrier, inc=1, device_id=device, device_id_type=pl.DeviceIdType.MESH)

    peers(nq, me, lambda o: greet((z, o)))
    peers(nb, z, lambda o: greet((o, me)))

    my_in = win_v.at[pl.ds(pl.multiple_of(core * hid, hid), hid)]
    my_out = wout_v.at[pl.ds(pl.multiple_of(core * hid, hid), hid)]
    ld_slots = pltpu.make_async_copy(slots_hbm, slots_v, ld_sem.at[0])
    ld_pos = pltpu.make_async_copy(pos_hbm, pos_v, ld_sem.at[1])
    ld_x = pltpu.make_async_copy(x_hbm, x_v, ld_sem.at[2])
    ld_in = pltpu.make_async_copy(win_hbm, my_in, ld_sem.at[3])
    ld_out = pltpu.make_async_copy(wout_hbm, my_out, ld_sem.at[4])
    ld_q = pltpu.make_async_copy(q_hbm, q_v.at[core, chip], ld_sem.at[5])
    for load in (ld_slots, ld_pos, ld_x, ld_in, ld_out, ld_q):
        load.start()

    def ld_k(c):
        part = pl.ds(pl.multiple_of(c * width, width), width)
        return pltpu.make_async_copy(k_hbm.at[part], k_ref.at[part], k_sem.at[c])

    for c in range(nch):
        ld_k(c).start()

    ld_slots.wait()
    eye = iota((lanes, lanes), 0) == iota((lanes, lanes), 1)
    slot_shift = seg.bit_length() - 1
    block_shift = blocks.bit_length() - 1
    owner_all = lax.shift_right_logical(slots_v[...], slot_shift)
    local = jnp.where(owner_all == me, slots_v[...] - me * seg, 0)
    slot_rows = slots_v.shape[0]
    per_row = lanes // blocks
    spread = (
        lax.shift_right_logical(iota((fresh, slot_rows), 0), per_row.bit_length() - 1)
        == iota((fresh, slot_rows), 1)
    )
    spread = jnp.where(spread, 1.0, 0.0).astype(BF16)
    in_group = lax.shift_right_logical(iota((fresh, lanes), 1), block_shift) == (
        iota((fresh, lanes), 0) & (per_row - 1)
    )
    high = dot(spread, lax.shift_right_logical(local, 6).astype(F32).astype(BF16))
    low = dot(spread, (local & 63).astype(F32).astype(BF16))
    high = jnp.where(in_group, high, 0.0)
    low = jnp.where(in_group, low, 0.0)
    off_col = jnp.sum(high * 64.0 + low, axis=1, keepdims=True)
    ones = jnp.ones((8, lanes), BF16)
    offrow_v[...] = nt_dot(ones, high.astype(BF16)) * 64.0 + nt_dot(ones, low.astype(BF16))

    def mark(c, carry):
        ids = (iota((1, width), 1) + c * width).astype(F32)
        hit = jnp.sum(jnp.where(off_col == ids, 1.0, 0.0), axis=0, keepdims=True)
        slot_v[c] = jnp.where(hit > 0.5, -0.5, ids)
        return carry

    lax.fori_loop(0, nch, mark, 0)

    ld_pos.wait()
    pos_local = (pos_v[...] - me * seg).astype(F32)
    for a in range(ques // lanes):
        col = row_to_col(pos_local[a : a + 1, :], eye)
        for u in range(lanes // qrows):
            there = a * (lanes // qrows) + u
            lp_v[there % CORES, there // CORES] = jnp.broadcast_to(
                col[u * qrows : (u + 1) * qrows], (qrows, lanes)
            )

    z_rows = rows // lanes
    z_slots = slots_v[pl.ds(pl.multiple_of(z * z_rows, z_rows), z_rows), :]
    z_owner = lax.shift_right_logical(z_slots, slot_shift)

    def selection(h):
        i = iota((chips * sub, lanes), 0)
        sub_shift = sub.bit_length() - 1
        owner = lax.shift_right_logical(i, sub_shift) * CORES + core
        code = owner * blocks + (i & (sub - 1)) + h * sub
        pieces = []
        for r in range(z_rows):
            block = lax.shift_right_logical(iota((1, lanes), 1) + r * lanes, block_shift)
            pieces.append(
                jnp.where(code == z_owner[r : r + 1, :] * blocks + block, 1.0, 0.0).astype(BF16)
            )
        return jnp.concatenate(pieces, axis=1)

    ld_q.wait()
    pl.semaphore_wait(barrier, nq - 1 + nb - 1)

    w_copies = [
        rcopy(win_hbm, my_in, w_send.at[0], w_recv.at[0], mate),
        rcopy(wout_hbm, my_out, w_send.at[1], w_recv.at[1], mate),
    ]
    for copy in w_copies:
        copy.start()

    def q_copy(slot, target, index):
        return rcopy(
            q_hbm, q_v.at[core, slot], q_send.at[index], q_recv.at[slot], same_core(target)
        )

    peers(chips, chip, lambda j: q_copy(chip, j, j).start())

    ld_x.wait()
    ld_in.wait()
    ld_out.wait()

    def p_copy(h, slot, target, index):
        return rcopy(
            part_v.at[h, target],
            precv_v.at[h, slot],
            p_send.at[h, index],
            p_recv.at[h, slot],
            same_core(target),
        )

    for h in range(HALVES):
        chosen = dot(selection(h), x_v[...]).astype(BF16)
        if h == 0:
            for copy in w_copies:
                copy.wait_recv()
        hidden = jax.nn.gelu(nt_dot(chosen, win_v[...])).astype(BF16)
        part = dot(hidden, wout_v[...])
        part_v[h] = part.astype(BF16).reshape(chips, sub, dim)
        peers(chips, chip, lambda j: p_copy(h, chip, j, j).start())

    peers(chips, chip, lambda j: q_copy(j, j, j).wait_recv())
    qp_out = rcopy(q_v.at[core], q_v.at[core], qp_sem.at[0], qp_sem.at[1], mate)
    qp_in = rcopy(q_v.at[1 - core], q_v.at[1 - core], qp_sem.at[0], qp_sem.at[1], mate)
    qp_out.start()

    def old_logits(g, first):
        q = q_v[g].reshape(half_q, dim)
        lp = lp_v[g].reshape(half_q, lanes)[:, 0:1]
        pp_v[g] = jnp.zeros((half_q, dim), F32)
        mx_v[g] = jnp.full((half_q, lanes), NEG, F32)

        def one(c, carry):
            if first:
                ld_k(c).wait()
            keys = k_ref[pl.ds(pl.multiple_of(c * width, width), width), :]
            ids = slot_v[c]
            logit = jnp.where(ids >= 0.0, nt_dot(q, keys) * scale2, NEG)
            s_v[c, g] = logit
            top = logit[:, 0:lanes]
            for t in range(1, width // lanes):
                top = jnp.maximum(top, logit[:, t * lanes : (t + 1) * lanes])
            mx_v[g] = jnp.maximum(mx_v[g], top)
            pick = jnp.where(lp == ids, 1.0, 0.0).astype(BF16)
            pp_v[g] += dot(pick, keys)
            return carry

        lax.fori_loop(0, nch, one, 0)

    def z_copy(h, slot, target, index):
        return rcopy(
            nk_v.at[slot, h], nk_v.at[slot, h], z_send.at[h, index], z_recv.at[h, slot], (target, me)
        )

    def finish_keys(h):
        peers(chips, chip, lambda j: p_copy(h, j, j, j).wait_recv())

        def add(d, total):
            return total + precv_v[h, lax.rem(chip + d, chips)].astype(F32)

        total = lax.fori_loop(1, chips, add, part_v[h, chip].astype(F32))
        norm = lax.rsqrt(jnp.sum(total * total, axis=1, keepdims=True) + epsilon)
        nk_v[z, h] = (total * norm).astype(BF16)
        peers(nb, z, lambda o: z_copy(h, z, o, o).start())

    old_logits(core, True)
    finish_keys(0)
    qp_in.wait_recv()
    old_logits(1 - core, False)
    finish_keys(1)

    m_old = jnp.max(mx_v[...].reshape(ques, lanes), axis=1, keepdims=True)
    acc_v[...] = jnp.zeros(acc_v.shape, F32)
    mx_v[...] = jnp.zeros(mx_v.shape, F32)

    def old_product(c, carry):
        keys = k_ref[pl.ds(pl.multiple_of(c * width, width), width), :]
        weight = jnp.exp2(s_v[c].reshape(ques, width) - m_old)
        total = weight[:, 0:lanes]
        for t in range(1, width // lanes):
            total = total + weight[:, t * lanes : (t + 1) * lanes]
        mx_v[...] += total.reshape(mx_v.shape)
        acc_v[...] += dot(weight.astype(BF16), keys).reshape(acc_v.shape)
        return carry

    lax.fori_loop(0, nch, old_product, 0)
    l_old = jnp.sum(mx_v[...].reshape(ques, lanes), axis=1, keepdims=True)

    for h in range(HALVES):
        peers(nb, z, lambda o: z_copy(h, o, o, o).wait_recv())
    fresh_keys = nk_v[...].reshape(fresh, dim)
    q_all = q_v[...].reshape(ques, dim)
    new_logit = nt_dot(q_all, fresh_keys) * scale2
    m_all = jnp.maximum(m_old, jnp.max(new_logit, axis=1, keepdims=True))
    new_weight = jnp.exp2(new_logit - m_all)
    fade = jnp.exp2(m_old - m_all)
    l_all = l_old * fade + jnp.sum(new_weight, axis=1, keepdims=True)
    groups = ques // lanes
    for a in range(groups):
        stats_v[me, a : a + 1, :] = col_to_row(m_all[a * lanes : (a + 1) * lanes], eye)
        stats_v[me, groups + a : groups + a + 1, :] = col_to_row(
            l_all[a * lanes : (a + 1) * lanes], eye
        )

    def st_copy(slot, target, index):
        return rcopy(
            stats_v.at[slot], stats_v.at[slot], st_send.at[index], st_recv.at[slot], (z, target)
        )

    peers(nq, me, lambda o: st_copy(me, o, o).start())

    acc = acc_v[...].reshape(ques, dim) * fade + dot(new_weight.astype(BF16), fresh_keys)
    acc_v[...] = acc.reshape(acc_v.shape)
    lp_all = lp_v[...].reshape(ques, lanes)[:, 0:1]
    pick_new = jnp.where(lp_all == offrow_v[0:1, :], 1.0, 0.0).astype(BF16)
    pos_rows = pp_v[...].reshape(ques, dim) + dot(pick_new, fresh_keys)
    pp_v[...] = pos_rows.reshape(pp_v.shape)
    pos_sum = jnp.sum(jnp.sum(q_all.astype(F32) * pos_rows, axis=0, keepdims=True)) * scale2

    def update(c, carry):
        part = pl.ds(pl.multiple_of(c * width, width), width)
        ids = (iota((width, fresh), 0) + c * width).astype(F32)
        place = jnp.where(ids == offrow_v[0:1, :], 1.0, 0.0)
        hit = jnp.sum(place, axis=1, keepdims=True) > 0.5
        moved = dot(place.astype(BF16), fresh_keys)
        k_ref[part, :] = jnp.where(hit, moved, k_ref[part, :].astype(F32)).astype(BF16)
        return carry

    lax.fori_loop(0, nch // 2, update, 0)

    peers(nq, me, lambda o: st_copy(o, o, o).wait_recv())
    top = stats_v[0, 0:groups, :]
    for o in range(1, nq):
        top = jnp.maximum(top, stats_v[o, 0:groups, :])
    total = jnp.zeros_like(top)
    for o in range(nq):
        total = total + stats_v[o, groups : 2 * groups, :] * jnp.exp2(
            stats_v[o, 0:groups, :] - top
        )
    log_total = top + jnp.log(total) * log2e
    share = jnp.exp2(stats_v[me, 0:groups, :] - log_total) * inverse_temp
    for a in range(groups):
        col = row_to_col(share[a : a + 1, :], eye)
        first = a * lanes // half_q
        start = a * lanes - first * half_q
        sc_v[first, start : start + lanes, :] = jnp.broadcast_to(col, (lanes, lanes))
    own_loss = jnp.sum(log_total) * (1.0 / nq) - pos_sum
    l1_v[z] = jnp.broadcast_to(own_loss, (1, lanes))

    def l1_copy(slot, target, index):
        return rcopy(l1_v.at[slot], l1_v.at[slot], l1_send.at[index], l1_recv.at[slot], (target, me))

    def term(g):
        return acc_v[g] * sc_v[g][:, 0:1] - inverse_temp * pp_v[g]

    psend_v[...] = term(1 - core)
    pair = rcopy(psend_v, pairr_v, gp_sem.at[0], gp_sem.at[1], mate)
    pair.start()
    peers(nb, z, lambda o: l1_copy(z, o, o).start())
    acc_v[core] = term(core)
    pair.wait_recv()
    both = acc_v[core] + pairr_v[...]
    acc_v[core] = both
    gsend_v[...] = both.astype(BF16).reshape(gsend_v.shape)

    def g_copy(slot, target, index):
        return rcopy(
            gsend_v.at[target], grecv_v.at[slot], g_send.at[index], g_recv.at[slot],
            same_core(target),
        )

    peers(chips, chip, lambda j: g_copy(chip, j, j).start())

    peers(nb, z, lambda o: l1_copy(o, o, o).wait_recv())
    l2_v[me] = jnp.sum(l1_v[...], axis=0)

    def l2_copy(slot, target, index):
        return rcopy(l2_v.at[slot], l2_v.at[slot], l2_send.at[index], l2_recv.at[slot], (z, target))

    peers(nq, me, lambda o: l2_copy(me, o, o).start())

    lax.fori_loop(nch // 2, nch, update, 0)

    peers(chips, chip, lambda j: g_copy(j, j, j).wait_recv())

    def add_grads(d, total):
        return total + grecv_v[lax.rem(chip + d, chips)].astype(F32)

    own = acc_v[core, pl.ds(pl.multiple_of(chip * qrows, qrows), qrows), :]
    grads_ref[...] = lax.fori_loop(1, chips, add_grads, own)
    peers(nq, me, lambda o: l2_copy(o, o, o).wait_recv())
    loss_ref[...] = jnp.sum(l2_v[...], axis=0) * (1.0 / (log2e * ques * nb))

    for copy in w_copies:
        copy.wait_send()
    qp_out.wait_send()
    pair.wait_send()
    peers(chips, chip, lambda j: q_copy(chip, j, j).wait_send())
    for h in range(HALVES):
        peers(chips, chip, lambda j: p_copy(h, chip, j, j).wait_send())
        peers(nb, z, lambda o: z_copy(h, z, o, o).wait_send())
    peers(nq, me, lambda o: st_copy(me, o, o).wait_send())
    peers(chips, chip, lambda j: g_copy(chip, j, j).wait_send())
    peers(nb, z, lambda o: l1_copy(z, o, o).wait_send())
    peers(nq, me, lambda o: l2_copy(me, o, o).wait_send())


def body(key_inputs, head_in, head_out, queue_keys, slots, questions, positives):
    nb = lax.axis_size("batch")
    nq = lax.axis_size("queue")
    chips = nq // CORES
    rows, dim = key_inputs.shape
    hid = head_in.shape[0]
    seg = queue_keys.shape[0]
    qrows = questions.shape[0]
    half_q = chips * qrows
    ques = nq * qrows
    blocks = rows // nq
    sub = blocks // HALVES
    fresh = nb * blocks
    lanes = 128
    nch = 4
    width = seg // nch
    any_spec = pl.BlockSpec(memory_space=pl.ANY)
    vmem_spec = pl.BlockSpec(memory_space=pltpu.VMEM)
    dma = pltpu.SemaphoreType.DMA
    v = pltpu.VMEM
    queue_out, loss, grads = pl.pallas_call(
        functools.partial(kernel, nb, nq),
        out_shape=(
            jax.ShapeDtypeStruct((seg, dim), BF16),
            jax.ShapeDtypeStruct((1, lanes), F32),
            jax.ShapeDtypeStruct((qrows, dim), F32),
        ),
        in_specs=[any_spec] * 7,
        out_specs=(vmem_spec,) * 3,
        scratch_shapes=[
            v((nb * rows // lanes, lanes), jnp.int32),
            v((ques // lanes, lanes), jnp.int32),
            v((rows, dim), BF16),
            v((CORES * hid, dim), BF16),
            v((CORES * hid, dim), BF16),
            v((HALVES, chips, sub, dim), BF16),
            v((HALVES, chips, sub, dim), BF16),
            v((CORES, chips, qrows, dim), BF16),
            v((nb, HALVES, sub, dim), BF16),
            v((nch, CORES, half_q, width), F32),
            v((CORES, half_q, dim), F32),
            v((CORES, half_q, dim), F32),
            v((CORES, half_q, lanes), F32),
            v((nch, 1, width), F32),
            v((8, fresh), F32),
            v((CORES, chips, qrows, lanes), F32),
            v((CORES, half_q, lanes), F32),
            v((nq, 2 * ques // lanes, lanes), F32),
            v((half_q, dim), F32),
            v((half_q, dim), F32),
            v((chips, qrows, dim), BF16),
            v((chips, qrows, dim), BF16),
            v((nb, 1, lanes), F32),
            v((nq, 1, lanes), F32),
            dma((6,)),
            dma((nch,)),
            dma((2,)),
            dma((2,)),
            dma((chips,)),
            dma((chips,)),
            dma((2,)),
            dma((HALVES, chips)),
            dma((HALVES, chips)),
            dma((HALVES, nb)),
            dma((HALVES, nb)),
            dma((nq,)),
            dma((nq,)),
            dma((2,)),
            dma((chips,)),
            dma((chips,)),
            dma((nb,)),
            dma((nb,)),
            dma((nq,)),
            dma((nq,)),
        ],
        compiler_params=pltpu.CompilerParams(
            collective_id=0, has_side_effects=True, vmem_limit_bytes=58 * 1024 * 1024
        ),
        name="queue_step",
    )(
        key_inputs,
        head_in,
        head_out,
        queue_keys,
        slots.reshape(-1, lanes),
        questions,
        positives.reshape(-1, lanes),
    )
    return (queue_out, loss[0, 0], grads)


def solution(mesh):
    placed = (
        P("batch", None),
        P("queue", None),
        P("queue", None),
        P("queue", None),
        P(),
        P(("batch", "queue"), None),
        P("batch"),
    )
    return jax.shard_map(
        body,
        mesh=mesh,
        in_specs=placed,
        out_specs=(P("queue", None), P(), P(("batch", "queue"), None)),
        check_vma=False,
    )
```

time: 441 us -> 83.3 us (0.19)
  blocking collectives: 163 us -> 0 us
  waiting for transfers between devices: 104 us -> 0 us
  other arithmetic: 73.6 us -> 0 us
  Pallas kernels: 0 us -> 72.9 us
  local copies, waits for them, and re-layouts: 52.7 us -> 8.43 us
  matrix products: 23.2 us -> 0 us
  between operations: 15.8 us -> 1.84 us
  starting transfers between devices: 7.42 us -> 0 us
    reduce_scatter x2 -> x0, waiting for transfers between devices: 94.2 us -> none  [the longest x1 66.4 us: body(): lax.psum_scatter(inverse_temp * (product - jnp.where(inside[:, None], pos...]
    psum x2 -> x0, blocking collectives: 75.7 us -> none  [the longest x1 63 us: body(): lax.psum((jnp.sum(jnp.exp(logits - row_top[:, None]), axis=1), pos_part),...]
    pallas_call x0 -> x1, Pallas kernels: none -> 72.9 us  [body(): pl.pallas_call(functools.partial(kernel, nb, nq), out_shape=(jax.ShapeDty...]
    pmax x1 -> x0, blocking collectives: 66.4 us -> none  [body(): row_top = lax.pmax(local_top, 'queue')]
    scatter-add x1 -> x0, other arithmetic: 57 us -> none  [body(): jnp.nonzero(slots // seg_len == own_index, size=incoming.shape[0])[0]]
    gather x4 -> x0, local copies, waits for them, and re-layouts: 31.7 us -> none  [the longest x1 22.1 us: body(): picked = jnp.take_along_axis(logits, clipped[:, None], axis=1)[:, 0]]
    dot_general x3 -> x0, matrix products: 23.2 us -> none  [the longest x1 11.7 us: body(): product = jnp.dot(weights, queue_out, preferred_element_type=jnp.float32)]
    all_gather x1 -> x0, blocking collectives: 21.3 us -> none  [body(): incoming = lax.all_gather(arrived, 'batch', axis=0, tiled=True)]
  transfers between devices with their start and end apart: 4 -> 0, of which waited for: 4 -> 0; matrix products, arithmetic and copies ran while one was open for 18% -> 0% of each run, Pallas kernels for 0% -> 0%
where the time goes in v1:
time: 83.3 us; the launch traced here: 83.2 us
  Pallas kernels  72.9 us (88%)
  local copies, waits for them, and re-layouts  8.43 us (10%)
  between operations  1.84 us (2%)
    pallas_call x1, Pallas kernels, body(): pl.pallas_call(functools.partial(kernel, nb, nq), out_shape=(jax.ShapeDty...  72.9 us
    unnamed x6, local copies, waits for them, and re-layouts  8.43 us

profile of v1, /device:TPU:1, one launch (start us, length us, event | category | flops | bytes accessed | tf_op | source)
XLA Modules:
  0.0 83.2 jit_solution(11129338034677754206)
XLA Ops:
  0.6 72.9 %queue_step.1 = (bf16[4096,1024]{1,0:T(8,128)(2,1)}, f32[1,128]{1,0:T(1,128)}, f32[16,1024]{1,0:T(8,128)}) custom-call(bf16[1024,1024]{1,0:T(8,128)(2,1)} %x_hbm.1, bf16[128,1024]{1,0:T(8,128)(2,1)} %win_hbm.1, bf16[128,1024]{1,0:T(8,128)(2,1)} %wout_hbm.1, bf16[4096,1024]{1,0:T(8,128)(2,1)} %k_hbm.1, s32[64,128]{1,0:T(8,128)} %bitcast.4, ...), custom_call_target="tpu_custom_call" | custom-call | tf_op jit(solution)/shard_map/queue_step/pallas_call | solution.py:423
  73.5 0.0 copy-start.1
  73.6 0.0 copy-start
  73.6 7.8 %copy.13 = bf16[4096,1024]{1,0:T(8,128)(2,1)} copy(bf16[4096,1024]{1,0:T(8,128)(2,1)} %get-tuple-element.12) | data formatting | bytes 16777216
  81.4 0.0 copy-done.1
  81.4 0.0 copy-done
  81.4 0.6 copy.15
Async XLA Ops:
  73.5 7.8 %copy-start.1 = (f32[1,128]{1,0:T(1,128)S(1)}, f32[1,128]{1,0:T(1,128)}, u32[]{:S(2)}) copy-start(f32[1,128]{1,0:T(1,128)} %get-tuple-element.7) | copy-start | bytes 1540
  73.6 7.8 %copy-start = (f32[16,1024]{1,0:T(8,128)S(1)}, f32[16,1024]{1,0:T(8,128)}, u32[]{:S(2)}) copy-start(f32[16,1024]{1,0:T(8,128)} %get-tuple-element.14) | copy-start | bytes 196612

commit v2 on v1

--- a/solution.py
+++ b/solution.py
@@ -14,6 +14,8 @@
 F32 = jnp.float32
 BF16 = jnp.bfloat16
 NEG = -1e30
+STEPS = 32700.0
+TINY = 1e-30
 CORES = 2
 HALVES = 2
 
@@ -62,9 +64,9 @@
     x_hbm, win_hbm, wout_hbm, k_hbm, slots_hbm, q_hbm, pos_hbm,
     k_ref, loss_ref, grads_ref,
     slots_v, pos_v, x_v, win_v, wout_v, part_v, precv_v, q_v, nk_v, s_v, acc_v, pp_v,
-    mx_v, slot_v, offrow_v, lp_v, sc_v, stats_v, psend_v, pairr_v, gsend_v, grecv_v, l1_v, l2_v,
+    mx_v, slot_v, offrow_v, lp_v, sc_v, stats_v, psend_v, pairr_v, gsend_v, grecv_v, l1_v, l2_v, sel_v,
     ld_sem, k_sem, w_send, w_recv, q_send, q_recv, qp_sem, p_send, p_recv, z_send, z_recv,
-    st_send, st_recv, gp_sem, g_send, g_recv, l1_send, l1_recv, l2_send, l2_recv,
+    st_send, st_recv, gp_send, gp_recv, g_send, g_recv, l1_send, l1_recv, l2_send, l2_recv,
 ):
     z = lax.axis_index("batch")
     me = lax.axis_index("queue")
@@ -174,6 +176,20 @@
             )
         return jnp.concatenate(pieces, axis=1)
 
+    ld_x.wait()
+    for h in range(HALVES):
+        sel_v[h] = dot(selection(h), x_v[...]).astype(BF16)
+    chosen = sel_v[...].reshape(HALVES * chips * sub, dim)
+
+    def head(index):
+        units = pl.ds(pl.multiple_of(index * hid, hid), hid)
+        hidden = jax.nn.gelu(nt_dot(chosen, win_v[units, :])).astype(BF16)
+        return dot(hidden, wout_v[units, :])
+
+    ld_in.wait()
+    ld_out.wait()
+    acc_v[...] = head(core).reshape(acc_v.shape)
+
     ld_q.wait()
     pl.semaphore_wait(barrier, nq - 1 + nb - 1)
 
@@ -190,10 +206,6 @@
         )
 
     peers(chips, chip, lambda j: q_copy(chip, j, j).start())
-
-    ld_x.wait()
-    ld_in.wait()
-    ld_out.wait()
 
     def p_copy(h, slot, target, index):
         return rcopy(
@@ -204,65 +216,106 @@
             same_core(target),
         )
 
+    for copy in w_copies:
+        copy.wait_recv()
+    part = acc_v[...].reshape(HALVES * chips * sub, dim) + head(1 - core)
+    most = jnp.maximum(jnp.max(jnp.abs(part), axis=1, keepdims=True), TINY)
+    exponent = jnp.ceil(jnp.log(most) * log2e)
+    coded = jnp.round(part * (jnp.exp2(-exponent) * STEPS)).astype(jnp.int32)
+    part_v[:, :, :, 0:dim] = coded.astype(jnp.int16).reshape(HALVES, chips, sub, dim)
+    tail = jnp.broadcast_to(exponent, (exponent.shape[0], lanes)).astype(jnp.int32)
+    part_v[:, :, :, dim : dim + lanes] = tail.astype(jnp.int16).reshape(HALVES, chips, sub, lanes)
     for h in range(HALVES):
-        chosen = dot(selection(h), x_v[...]).astype(BF16)
-        if h == 0:
-            for copy in w_copies:
-                copy.wait_recv()
-        hidden = jax.nn.gelu(nt_dot(chosen, win_v[...])).astype(BF16)
-        part = dot(hidden, wout_v[...])
-        part_v[h] = part.astype(BF16).reshape(chips, sub, dim)
         peers(chips, chip, lambda j: p_copy(h, chip, j, j).start())
+
+    lp_all = lp_v[...].reshape(ques, lanes)[:, 0:1]
+    pp_v[...] = jnp.zeros(pp_v.shape, F32)
+
+    def old_rows(c, carry):
+        ld_k(c).wait()
+        keys = k_ref[pl.ds(pl.multiple_of(c * width, width), width), :]
+        pick = jnp.where(lp_all == slot_v[c], 1.0, 0.0).astype(BF16)
+        pp_v[...] += dot(pick, keys).reshape(pp_v.shape)
+        return carry
+
+    lax.fori_loop(0, nch - 1, old_rows, 0)
 
     peers(chips, chip, lambda j: q_copy(j, j, j).wait_recv())
     qp_out = rcopy(q_v.at[core], q_v.at[core], qp_sem.at[0], qp_sem.at[1], mate)
     qp_in = rcopy(q_v.at[1 - core], q_v.at[1 - core], qp_sem.at[0], qp_sem.at[1], mate)
     qp_out.start()
-
-    def old_logits(g, first):
+    old_rows(nch - 1, 0)
+
+    mx_v[...] = jnp.full(mx_v.shape, NEG, F32)
+
+    def old_logits(g, start, stop):
         q = q_v[g].reshape(half_q, dim)
-        lp = lp_v[g].reshape(half_q, lanes)[:, 0:1]
-        pp_v[g] = jnp.zeros((half_q, dim), F32)
-        mx_v[g] = jnp.full((half_q, lanes), NEG, F32)
 
         def one(c, carry):
-            if first:
-                ld_k(c).wait()
             keys = k_ref[pl.ds(pl.multiple_of(c * width, width), width), :]
-            ids = slot_v[c]
-            logit = jnp.where(ids >= 0.0, nt_dot(q, keys) * scale2, NEG)
+            logit = jnp.where(slot_v[c] >= 0.0, nt_dot(q, keys) * scale2, NEG)
             s_v[c, g] = logit
             top = logit[:, 0:lanes]
             for t in range(1, width // lanes):
                 top = jnp.maximum(top, logit[:, t * lanes : (t + 1) * lanes])
             mx_v[g] = jnp.maximum(mx_v[g], top)
-            pick = jnp.where(lp == ids, 1.0, 0.0).astype(BF16)
-            pp_v[g] += dot(pick, keys)
             return carry
 
-        lax.fori_loop(0, nch, one, 0)
-
-    def z_copy(h, slot, target, index):
+        lax.fori_loop(start, stop, one, 0)
+
+    right = (lax.rem(z + 1, nb), me)
+    left = (lax.rem(z + nb - 1, nb), me)
+    reach = [(nb // 2, nb - 1 - nb // 2), (nb - 1 - nb // 2, nb // 2)]
+
+    def z_copy(h, way, hop):
+        away = (hop - 1) if way else (nb - hop + 1)
+        slot = lax.rem(z + away, nb)
+        there = nk_v.at[slot, h]
         return rcopy(
-            nk_v.at[slot, h], nk_v.at[slot, h], z_send.at[h, index], z_recv.at[h, slot], (target, me)
-        )
+            there, there, z_send.at[h, way, hop - 1], z_recv.at[h, slot], left if way else right
+        )
+
+    def z_arrived(h, way, hop):
+        slot = lax.rem(z + (hop if way else nb - hop), nb)
+        there = nk_v.at[slot, h]
+        rcopy(there, there, z_send.at[h, way, hop - 1], z_recv.at[h, slot], right).wait_recv()
+
+    def z_step(h, hop):
+        for way in range(2):
+            if hop > 1 and hop - 1 <= reach[h][way]:
+                z_arrived(h, way, hop - 1)
+            if hop <= reach[h][way]:
+                z_copy(h, way, hop).start()
 
     def finish_keys(h):
         peers(chips, chip, lambda j: p_copy(h, j, j, j).wait_recv())
 
+        def decoded(ref, j):
+            steps = ref[h, j, :, 0:dim].astype(jnp.int32).astype(F32)
+            exponents = ref[h, j, :, dim : dim + lanes].astype(jnp.int32).astype(F32)
+            return steps * (jnp.exp2(exponents[:, 0:1]) * (1.0 / STEPS))
+
         def add(d, total):
-            return total + precv_v[h, lax.rem(chip + d, chips)].astype(F32)
-
-        total = lax.fori_loop(1, chips, add, part_v[h, chip].astype(F32))
+            return total + decoded(precv_v, lax.rem(chip + d, chips))
+
+        total = lax.fori_loop(1, chips, add, decoded(part_v, chip))
         norm = lax.rsqrt(jnp.sum(total * total, axis=1, keepdims=True) + epsilon)
         nk_v[z, h] = (total * norm).astype(BF16)
-        peers(nb, z, lambda o: z_copy(h, z, o, o).start())
-
-    old_logits(core, True)
+
+    mid = nch // 2
+    old_logits(core, 0, mid)
     finish_keys(0)
+    z_step(0, 1)
+    old_logits(core, mid, nch)
+    z_step(0, 2)
     qp_in.wait_recv()
-    old_logits(1 - core, False)
+    old_logits(1 - core, 0, mid)
     finish_keys(1)
+    z_step(1, 1)
+    z_step(0, 3)
+    old_logits(1 - core, mid, nch)
+    z_step(1, 2)
+    z_step(0, 4)
 
     m_old = jnp.max(mx_v[...].reshape(ques, lanes), axis=1, keepdims=True)
     acc_v[...] = jnp.zeros(acc_v.shape, F32)
@@ -278,11 +331,16 @@
         acc_v[...] += dot(weight.astype(BF16), keys).reshape(acc_v.shape)
         return carry
 
-    lax.fori_loop(0, nch, old_product, 0)
+    old_product(0, 0)
+    z_step(1, 3)
+    z_step(0, 5)
+    old_product(1, 0)
+    z_step(1, 4)
+    old_product(2, 0)
+    z_step(1, 5)
+    lax.fori_loop(3, nch, old_product, 0)
     l_old = jnp.sum(mx_v[...].reshape(ques, lanes), axis=1, keepdims=True)
 
-    for h in range(HALVES):
-        peers(nb, z, lambda o: z_copy(h, o, o, o).wait_recv())
     fresh_keys = nk_v[...].reshape(fresh, dim)
     q_all = q_v[...].reshape(ques, dim)
     new_logit = nt_dot(q_all, fresh_keys) * scale2
@@ -306,7 +364,6 @@
 
     acc = acc_v[...].reshape(ques, dim) * fade + dot(new_weight.astype(BF16), fresh_keys)
     acc_v[...] = acc.reshape(acc_v.shape)
-    lp_all = lp_v[...].reshape(ques, lanes)[:, 0:1]
     pick_new = jnp.where(lp_all == offrow_v[0:1, :], 1.0, 0.0).astype(BF16)
     pos_rows = pp_v[...].reshape(ques, dim) + dot(pick_new, fresh_keys)
     pp_v[...] = pos_rows.reshape(pp_v.shape)
@@ -345,26 +402,38 @@
     def l1_copy(slot, target, index):
         return rcopy(l1_v.at[slot], l1_v.at[slot], l1_send.at[index], l1_recv.at[slot], (target, me))
 
-    def term(g):
-        return acc_v[g] * sc_v[g][:, 0:1] - inverse_temp * pp_v[g]
-
-    psend_v[...] = term(1 - core)
-    pair = rcopy(psend_v, pairr_v, gp_sem.at[0], gp_sem.at[1], mate)
-    pair.start()
+    def term(g, d):
+        part = pl.ds(pl.multiple_of(lax.rem(chip + d, chips) * qrows, qrows), qrows)
+        return acc_v[g, part, :] * sc_v[g, part, 0:1] - inverse_temp * pp_v[g, part, :]
+
+    def pair(half):
+        part = pl.ds(half * (chips // 2), chips // 2)
+        return rcopy(psend_v.at[part], pairr_v.at[part], gp_send.at[half], gp_recv.at[half], mate)
+
+    def fill(d, carry):
+        psend_v[d - 1] = term(1 - core, d)
+        return carry
+
+    for half in range(2):
+        lax.fori_loop(half * (chips // 2) + 1, (half + 1) * (chips // 2) + 1, fill, 0)
+        pair(half).start()
     peers(nb, z, lambda o: l1_copy(z, o, o).start())
-    acc_v[core] = term(core)
-    pair.wait_recv()
-    both = acc_v[core] + pairr_v[...]
-    acc_v[core] = both
-    gsend_v[...] = both.astype(BF16).reshape(gsend_v.shape)
-
-    def g_copy(slot, target, index):
+
+    def g_copy(d, target, slot):
         return rcopy(
-            gsend_v.at[target], grecv_v.at[slot], g_send.at[index], g_recv.at[slot],
+            gsend_v.at[d - 1], grecv_v.at[slot], g_send.at[d - 1], g_recv.at[slot],
             same_core(target),
         )
 
-    peers(chips, chip, lambda j: g_copy(chip, j, j).start())
+    def join(d, carry):
+        gsend_v[d - 1] = (term(core, d) + pairr_v[d - 1]).astype(BF16)
+        g_copy(d, lax.rem(chip + d, chips), chip).start()
+        return carry
+
+    pair(0).wait_recv()
+    lax.fori_loop(1, chips // 2 + 1, join, 0)
+    pair(1).wait_recv()
+    lax.fori_loop(chips // 2 + 1, chips, join, 0)
 
     peers(nb, z, lambda o: l1_copy(o, o, o).wait_recv())
     l2_v[me] = jnp.sum(l1_v[...], axis=0)
@@ -376,12 +445,12 @@
 
     lax.fori_loop(nch // 2, nch, update, 0)
 
-    peers(chips, chip, lambda j: g_copy(j, j, j).wait_recv())
+    peers(chips, chip, lambda j: g_copy(1, j, j).wait_recv())
 
     def add_grads(d, total):
         return total + grecv_v[lax.rem(chip + d, chips)].astype(F32)
 
-    own = acc_v[core, pl.ds(pl.multiple_of(chip * qrows, qrows), qrows), :]
+    own = term(core, chips) + pairr_v[chips - 1]
     grads_ref[...] = lax.fori_loop(1, chips, add_grads, own)
     peers(nq, me, lambda o: l2_copy(o, o, o).wait_recv())
     loss_ref[...] = jnp.sum(l2_v[...], axis=0) * (1.0 / (log2e * ques * nb))
@@ -389,13 +458,21 @@
     for copy in w_copies:
         copy.wait_send()
     qp_out.wait_send()
-    pair.wait_send()
+    for half in range(2):
+        pair(half).wait_send()
     peers(chips, chip, lambda j: q_copy(chip, j, j).wait_send())
     for h in range(HALVES):
         peers(chips, chip, lambda j: p_copy(h, chip, j, j).wait_send())
-        peers(nb, z, lambda o: z_copy(h, z, o, o).wait_send())
+        for way in range(2):
+            for hop in range(1, reach[h][way] + 1):
+                z_copy(h, way, hop).wait_send()
     peers(nq, me, lambda o: st_copy(me, o, o).wait_send())
-    peers(chips, chip, lambda j: g_copy(chip, j, j).wait_send())
+
+    def g_left(d, carry):
+        g_copy(d, lax.rem(chip + d, chips), chip).wait_send()
+        return carry
+
+    lax.fori_loop(1, chips, g_left, 0)
     peers(nb, z, lambda o: l1_copy(z, o, o).wait_send())
     peers(nq, me, lambda o: l2_copy(me, o, o).wait_send())
 
@@ -423,7 +500,7 @@
     queue_out, loss, grads = pl.pallas_call(
         functools.partial(kernel, nb, nq),
         out_shape=(
-            jax.ShapeDtypeStruct((seg, dim), BF16),
+            pltpu.VMEM((seg, dim), BF16),
             jax.ShapeDtypeStruct((1, lanes), F32),
             jax.ShapeDtypeStruct((qrows, dim), F32),
         ),
@@ -435,8 +512,8 @@
             v((rows, dim), BF16),
             v((CORES * hid, dim), BF16),
             v((CORES * hid, dim), BF16),
-            v((HALVES, chips, sub, dim), BF16),
-            v((HALVES, chips, sub, dim), BF16),
+            v((HALVES, chips, sub, dim + lanes), jnp.int16),
+            v((HALVES, chips, sub, dim + lanes), jnp.int16),
             v((CORES, chips, qrows, dim), BF16),
             v((nb, HALVES, sub, dim), BF16),
             v((nch, CORES, half_q, width), F32),
@@ -448,12 +525,13 @@
             v((CORES, chips, qrows, lanes), F32),
             v((CORES, half_q, lanes), F32),
             v((nq, 2 * ques // lanes, lanes), F32),
-            v((half_q, dim), F32),
-            v((half_q, dim), F32),
+            v((chips, qrows, dim), F32),
+            v((chips, qrows, dim), F32),
             v((chips, qrows, dim), BF16),
             v((chips, qrows, dim), BF16),
             v((nb, 1, lanes), F32),
             v((nq, 1, lanes), F32),
+            v((HALVES, chips * sub, dim), BF16),
             dma((6,)),
             dma((nch,)),
             dma((2,)),
@@ -463,10 +541,11 @@
             dma((2,)),
             dma((HALVES, chips)),
             dma((HALVES, chips)),
-            dma((HALVES, nb)),
+            dma((HALVES, 2, nb // 2)),
             dma((HALVES, nb)),
             dma((nq,)),
             dma((nq,)),
+            dma((2,)),
             dma((2,)),
             dma((chips,)),
             dma((chips,)),
@@ -476,7 +555,7 @@
             dma((nq,)),
         ],
         compiler_params=pltpu.CompilerParams(
-            collective_id=0, has_side_effects=True, vmem_limit_bytes=58 * 1024 * 1024
+            collective_id=0, has_side_effects=True, vmem_limit_bytes=54 * 1024 * 1024
         ),
         name="queue_step",
     )(

time: 83.3 us -> 83.3 us (level)
  Pallas kernels: 72.9 us -> 77.3 us
  local copies, waits for them, and re-layouts: 8.43 us -> 4.04 us
    unnamed x6, local copies, waits for them, and re-layouts: 8.43 us -> 4.04 us
    pallas_call x1, Pallas kernels: 72.9 us -> 77.3 us  [body(): pl.pallas_call(functools.partial(kernel, nb, nq), out_shape=(pltpu.VMEM((...]
where the time goes in v2:
time: 83.3 us; the launch traced here: 83.2 us
  Pallas kernels  77.3 us (93%)
  local copies, waits for them, and re-layouts  4.04 us (5%)
  between operations  1.84 us (2%)
    pallas_call x1, Pallas kernels, body(): pl.pallas_call(functools.partial(kernel, nb, nq), out_shape=(pltpu.VMEM((...  77.3 us
    unnamed x6, local copies, waits for them, and re-layouts  4.04 us

profile of v2, /device:TPU:1, one launch (start us, length us, event | category | flops | bytes accessed | tf_op | source)
XLA Modules:
  0.0 83.2 jit_solution(8746806476905308363)
XLA Ops:
  0.6 77.3 %queue_step.1 = (bf16[4096,1024]{1,0:T(8,128)(2,1)S(1)}, f32[1,128]{1,0:T(1,128)}, f32[16,1024]{1,0:T(8,128)}) custom-call(bf16[1024,1024]{1,0:T(8,128)(2,1)} %x_hbm.1, bf16[128,1024]{1,0:T(8,128)(2,1)} %win_hbm.1, bf16[128,1024]{1,0:T(8,128)(2,1)} %wout_hbm.1, bf16[4096,1024]{1,0:T(8,128)(2,1)} %k_hbm.1, s32[64,128]{1,0:T(8,128)} %bitcast.4, ...), custom_call_target="tpu_custom_call" | custom-call | tf_op jit(solution)/shard_map/queue_step/pallas_call | solution.py:500
  77.9 0.0 copy-start.1
  77.9 0.0 copy-start
  77.9 3.4 %copy.13 = bf16[4096,1024]{1,0:T(8,128)(2,1)} copy(bf16[4096,1024]{1,0:T(8,128)(2,1)S(1)} %get-tuple-element.9) | data formatting | bytes 16777216
  81.3 0.0 copy-done.1
  81.4 0.0 copy-done
  81.4 0.6 copy.15
Async XLA Ops:
  77.9 3.4 %copy-start.1 = (f32[1,128]{1,0:T(1,128)S(1)}, f32[1,128]{1,0:T(1,128)}, u32[]{:S(2)}) copy-start(f32[1,128]{1,0:T(1,128)} %get-tuple-element.7) | copy-start | bytes 1540
  77.9 3.5 %copy-start = (f32[16,1024]{1,0:T(8,128)S(1)}, f32[16,1024]{1,0:T(8,128)}, u32[]{:S(2)}) copy-start(f32[16,1024]{1,0:T(8,128)} %get-tuple-element.17) | copy-start | bytes 196612

commit v3 on v2

--- a/solution.py
+++ b/solution.py
@@ -64,9 +64,10 @@
     x_hbm, win_hbm, wout_hbm, k_hbm, slots_hbm, q_hbm, pos_hbm,
     k_ref, loss_ref, grads_ref,
     slots_v, pos_v, x_v, win_v, wout_v, part_v, precv_v, q_v, nk_v, s_v, acc_v, pp_v,
-    mx_v, slot_v, offrow_v, lp_v, sc_v, stats_v, psend_v, pairr_v, gsend_v, grecv_v, l1_v, l2_v, sel_v,
+    mx_v, slot_v, offrow_v, lp_v, sc_v, stats_v, psend_v, pairr_v, gsend_v, grecv_v, l1_v, l2_v, sel_v, exp_v, hello_v,
     ld_sem, k_sem, w_send, w_recv, q_send, q_recv, qp_sem, p_send, p_recv, z_send, z_recv,
     st_send, st_recv, gp_send, gp_recv, g_send, g_recv, l1_send, l1_recv, l2_send, l2_recv,
+    e_send, e_recv, hello_send, hello_recv,
 ):
     z = lax.axis_index("batch")
     me = lax.axis_index("queue")
@@ -200,12 +201,20 @@
     for copy in w_copies:
         copy.start()
 
+    def hello(slot, target, index):
+        return rcopy(
+            hello_v.at[slot], hello_v.at[slot], hello_send.at[index], hello_recv.at[slot],
+            (target, me),
+        )
+
     def q_copy(slot, target, index):
         return rcopy(
             q_hbm, q_v.at[core, slot], q_send.at[index], q_recv.at[slot], same_core(target)
         )
 
     peers(chips, chip, lambda j: q_copy(chip, j, j).start())
+    hello_v[z] = jnp.zeros((1, lanes), F32)
+    peers(nb, z, lambda o: hello(z, o, o).start())
 
     def p_copy(h, slot, target, index):
         return rcopy(
@@ -222,9 +231,16 @@
     most = jnp.maximum(jnp.max(jnp.abs(part), axis=1, keepdims=True), TINY)
     exponent = jnp.ceil(jnp.log(most) * log2e)
     coded = jnp.round(part * (jnp.exp2(-exponent) * STEPS)).astype(jnp.int32)
-    part_v[:, :, :, 0:dim] = coded.astype(jnp.int16).reshape(HALVES, chips, sub, dim)
-    tail = jnp.broadcast_to(exponent, (exponent.shape[0], lanes)).astype(jnp.int32)
-    part_v[:, :, :, dim : dim + lanes] = tail.astype(jnp.int16).reshape(HALVES, chips, sub, lanes)
+    part_v[...] = coded.astype(jnp.int16).reshape(part_v.shape)
+    for a in range(exp_v.shape[1]):
+        exp_v[chip, a : a + 1, :] = col_to_row(exponent[a * lanes : (a + 1) * lanes], eye)
+
+    def e_copy(slot, target, index):
+        return rcopy(
+            exp_v.at[slot], exp_v.at[slot], e_send.at[index], e_recv.at[slot], same_core(target)
+        )
+
+    peers(chips, chip, lambda j: e_copy(chip, j, j).start())
     for h in range(HALVES):
         peers(chips, chip, lambda j: p_copy(h, chip, j, j).start())
 
@@ -263,37 +279,22 @@
 
         lax.fori_loop(start, stop, one, 0)
 
-    right = (lax.rem(z + 1, nb), me)
-    left = (lax.rem(z + nb - 1, nb), me)
-    reach = [(nb // 2, nb - 1 - nb // 2), (nb - 1 - nb // 2, nb // 2)]
-
-    def z_copy(h, way, hop):
-        away = (hop - 1) if way else (nb - hop + 1)
-        slot = lax.rem(z + away, nb)
+    def z_copy(h, slot, target, index):
         there = nk_v.at[slot, h]
-        return rcopy(
-            there, there, z_send.at[h, way, hop - 1], z_recv.at[h, slot], left if way else right
-        )
-
-    def z_arrived(h, way, hop):
-        slot = lax.rem(z + (hop if way else nb - hop), nb)
-        there = nk_v.at[slot, h]
-        rcopy(there, there, z_send.at[h, way, hop - 1], z_recv.at[h, slot], right).wait_recv()
-
-    def z_step(h, hop):
-        for way in range(2):
-            if hop > 1 and hop - 1 <= reach[h][way]:
-                z_arrived(h, way, hop - 1)
-            if hop <= reach[h][way]:
-                z_copy(h, way, hop).start()
+        return rcopy(there, there, z_send.at[h, index], z_recv.at[h, slot], (target, me))
 
     def finish_keys(h):
+        if h == 0:
+            peers(chips, chip, lambda j: e_copy(j, j, j).wait_recv())
         peers(chips, chip, lambda j: p_copy(h, j, j, j).wait_recv())
 
+        place = h * chips * sub + chip * sub
+        mine = iota((sub, lanes), 1) == iota((sub, lanes), 0) + lax.rem(place, lanes)
+
         def decoded(ref, j):
-            steps = ref[h, j, :, 0:dim].astype(jnp.int32).astype(F32)
-            exponents = ref[h, j, :, dim : dim + lanes].astype(jnp.int32).astype(F32)
-            return steps * (jnp.exp2(exponents[:, 0:1]) * (1.0 / STEPS))
+            row = exp_v[j, pl.ds(place // lanes, 1), :]
+            factor = jnp.exp2(row_to_col(row, mine)) * (1.0 / STEPS)
+            return ref[h, j].astype(jnp.int32).astype(F32) * factor
 
         def add(d, total):
             return total + decoded(precv_v, lax.rem(chip + d, chips))
@@ -301,21 +302,12 @@
         total = lax.fori_loop(1, chips, add, decoded(part_v, chip))
         norm = lax.rsqrt(jnp.sum(total * total, axis=1, keepdims=True) + epsilon)
         nk_v[z, h] = (total * norm).astype(BF16)
-
-    mid = nch // 2
-    old_logits(core, 0, mid)
+        peers(nb, z, lambda o: z_copy(h, z, o, o).start())
+
+    old_logits(core, 0, nch)
     finish_keys(0)
-    z_step(0, 1)
-    old_logits(core, mid, nch)
-    z_step(0, 2)
     qp_in.wait_recv()
-    old_logits(1 - core, 0, mid)
-    finish_keys(1)
-    z_step(1, 1)
-    z_step(0, 3)
-    old_logits(1 - core, mid, nch)
-    z_step(1, 2)
-    z_step(0, 4)
+    old_logits(1 - core, 0, nch)
 
     m_old = jnp.max(mx_v[...].reshape(ques, lanes), axis=1, keepdims=True)
     acc_v[...] = jnp.zeros(acc_v.shape, F32)
@@ -331,16 +323,14 @@
         acc_v[...] += dot(weight.astype(BF16), keys).reshape(acc_v.shape)
         return carry
 
-    old_product(0, 0)
-    z_step(1, 3)
-    z_step(0, 5)
-    old_product(1, 0)
-    z_step(1, 4)
-    old_product(2, 0)
-    z_step(1, 5)
-    lax.fori_loop(3, nch, old_product, 0)
+    mid = nch // 2
+    lax.fori_loop(0, mid, old_product, 0)
+    finish_keys(1)
+    lax.fori_loop(mid, nch, old_product, 0)
     l_old = jnp.sum(mx_v[...].reshape(ques, lanes), axis=1, keepdims=True)
 
+    for h in range(HALVES):
+        peers(nb, z, lambda o: z_copy(h, o, o, o).wait_recv())
     fresh_keys = nk_v[...].reshape(fresh, dim)
     q_all = q_v[...].reshape(ques, dim)
     new_logit = nt_dot(q_all, fresh_keys) * scale2
@@ -415,7 +405,8 @@
         return carry
 
     for half in range(2):
-        lax.fori_loop(half * (chips // 2) + 1, (half + 1) * (chips // 2) + 1, fill, 0)
+        first = half * (chips // 2) + 1
+        lax.fori_loop(first, first + chips // 2, fill, 0, unroll=4)
         pair(half).start()
     peers(nb, z, lambda o: l1_copy(z, o, o).start())
 
@@ -427,13 +418,18 @@
 
     def join(d, carry):
         gsend_v[d - 1] = (term(core, d) + pairr_v[d - 1]).astype(BF16)
+        return carry
+
+    def go(d, carry):
         g_copy(d, lax.rem(chip + d, chips), chip).start()
         return carry
 
     pair(0).wait_recv()
-    lax.fori_loop(1, chips // 2 + 1, join, 0)
+    lax.fori_loop(1, chips // 2 + 1, join, 0, unroll=4)
+    lax.fori_loop(1, chips // 2 + 1, go, 0)
     pair(1).wait_recv()
-    lax.fori_loop(chips // 2 + 1, chips, join, 0)
+    lax.fori_loop(chips // 2 + 1, chips + 1, join, 0, unroll=4)
+    lax.fori_loop(chips // 2 + 1, chips, go, 0)
 
     peers(nb, z, lambda o: l1_copy(o, o, o).wait_recv())
     l2_v[me] = jnp.sum(l1_v[...], axis=0)
@@ -461,11 +457,12 @@
     for half in range(2):
         pair(half).wait_send()
     peers(chips, chip, lambda j: q_copy(chip, j, j).wait_send())
+    peers(chips, chip, lambda j: e_copy(chip, j, j).wait_send())
+    peers(nb, z, lambda o: hello(z, o, o).wait_send())
+    peers(nb, z, lambda o: hello(o, o, o).wait_recv())
     for h in range(HALVES):
         peers(chips, chip, lambda j: p_copy(h, chip, j, j).wait_send())
-        for way in range(2):
-            for hop in range(1, reach[h][way] + 1):
-                z_copy(h, way, hop).wait_send()
+        peers(nb, z, lambda o: z_copy(h, z, o, o).wait_send())
     peers(nq, me, lambda o: st_copy(me, o, o).wait_send())
 
     def g_left(d, carry):
@@ -512,8 +509,8 @@
             v((rows, dim), BF16),
             v((CORES * hid, dim), BF16),
             v((CORES * hid, dim), BF16),
-            v((HALVES, chips, sub, dim + lanes), jnp.int16),
-            v((HALVES, chips, sub, dim + lanes), jnp.int16),
+            v((HALVES, chips, sub, dim), jnp.int16),
+            v((HALVES, chips, sub, dim), jnp.int16),
             v((CORES, chips, qrows, dim), BF16),
             v((nb, HALVES, sub, dim), BF16),
             v((nch, CORES, half_q, width), F32),
@@ -532,6 +529,8 @@
             v((nb, 1, lanes), F32),
             v((nq, 1, lanes), F32),
             v((HALVES, chips * sub, dim), BF16),
+            v((chips, HALVES * chips * sub // lanes, lanes), F32),
+            v((nb, 1, lanes), F32),
             dma((6,)),
             dma((nch,)),
             dma((2,)),
@@ -541,7 +540,7 @@
             dma((2,)),
             dma((HALVES, chips)),
             dma((HALVES, chips)),
-            dma((HALVES, 2, nb // 2)),
+            dma((HALVES, nb)),
             dma((HALVES, nb)),
             dma((nq,)),
             dma((nq,)),
@@ -553,6 +552,10 @@
             dma((nb,)),
             dma((nq,)),
             dma((nq,)),
+            dma((chips,)),
+            dma((chips,)),
+            dma((nb,)),
+            dma((nb,)),
         ],
         compiler_params=pltpu.CompilerParams(
             collective_id=0, has_side_effects=True, vmem_limit_bytes=54 * 1024 * 1024

time: 83.3 us -> 78.6 us (0.944)
  Pallas kernels: 77.3 us -> 72.7 us
    pallas_call x1, Pallas kernels: 77.3 us -> 72.7 us  [body(): pl.pallas_call(functools.partial(kernel, nb, nq), out_shape=(pltpu.VMEM((...]
where the time goes in v3:
time: 78.6 us; the launch traced here: 78.5 us
  Pallas kernels  72.7 us (92%)
  local copies, waits for them, and re-layouts  4.04 us (5%)
  between operations  1.84 us (2%)
    pallas_call x1, Pallas kernels, body(): pl.pallas_call(functools.partial(kernel, nb, nq), out_shape=(pltpu.VMEM((...  72.7 us
    unnamed x6, local copies, waits for them, and re-layouts  4.04 us

profile of v3, /device:TPU:1, one launch (start us, length us, event | category | flops | bytes accessed | tf_op | source)
XLA Modules:
  0.0 78.5 jit_solution(16452554393828895048)
XLA Ops:
  0.6 72.7 %queue_step.1 = (bf16[4096,1024]{1,0:T(8,128)(2,1)S(1)}, f32[1,128]{1,0:T(1,128)}, f32[16,1024]{1,0:T(8,128)}) custom-call(bf16[1024,1024]{1,0:T(8,128)(2,1)} %x_hbm.1, bf16[128,1024]{1,0:T(8,128)(2,1)} %win_hbm.1, bf16[128,1024]{1,0:T(8,128)(2,1)} %wout_hbm.1, bf16[4096,1024]{1,0:T(8,128)(2,1)} %k_hbm.1, s32[64,128]{1,0:T(8,128)} %bitcast.4, ...), custom_call_target="tpu_custom_call" | custom-call | tf_op jit(solution)/shard_map/queue_step/pallas_call | solution.py:497
  73.3 0.0 copy-start.1
  73.3 0.0 copy-start
  73.3 3.4 %copy.13 = bf16[4096,1024]{1,0:T(8,128)(2,1)} copy(bf16[4096,1024]{1,0:T(8,128)(2,1)S(1)} %get-tuple-element.9) | data formatting | bytes 16777216
  76.7 0.0 copy-done.1
  76.8 0.0 copy-done
  76.8 0.6 copy.15
Async XLA Ops:
  73.3 3.4 %copy-start.1 = (f32[1,128]{1,0:T(1,128)S(1)}, f32[1,128]{1,0:T(1,128)}, u32[]{:S(2)}) copy-start(f32[1,128]{1,0:T(1,128)} %get-tuple-element.7) | copy-start | bytes 1540
  73.3 3.5 %copy-start = (f32[16,1024]{1,0:T(8,128)S(1)}, f32[16,1024]{1,0:T(8,128)}, u32[]{:S(2)}) copy-start(f32[16,1024]{1,0:T(8,128)} %get-tuple-element.17) | copy-start | bytes 196612

commit v4 on v3

--- a/solution.py
+++ b/solution.py
@@ -323,10 +323,8 @@
         acc_v[...] += dot(weight.astype(BF16), keys).reshape(acc_v.shape)
         return carry
 
-    mid = nch // 2
-    lax.fori_loop(0, mid, old_product, 0)
     finish_keys(1)
-    lax.fori_loop(mid, nch, old_product, 0)
+    lax.fori_loop(0, nch, old_product, 0)
     l_old = jnp.sum(mx_v[...].reshape(ques, lanes), axis=1, keepdims=True)
 
     for h in range(HALVES):

time: 78.6 us -> 77.6 us (0.987)
  Pallas kernels: 72.7 us -> 71.6 us
    pallas_call x1, Pallas kernels: 72.7 us -> 71.6 us  [body(): pl.pallas_call(functools.partial(kernel, nb, nq), out_shape=(pltpu.VMEM((...]
where the time goes in v4:
time: 77.6 us; the launch traced here: 77.5 us
  Pallas kernels  71.6 us (92%)
  local copies, waits for them, and re-layouts  4.04 us (5%)
  between operations  1.84 us (2%)
    pallas_call x1, Pallas kernels, body(): pl.pallas_call(functools.partial(kernel, nb, nq), out_shape=(pltpu.VMEM((...  71.6 us
    unnamed x6, local copies, waits for them, and re-layouts  4.04 us

profile of v4, /device:TPU:1, one launch (start us, length us, event | category | flops | bytes accessed | tf_op | source)
XLA Modules:
  0.0 77.5 jit_solution(8725507060675254690)
XLA Ops:
  0.6 71.6 %queue_step.1 = (bf16[4096,1024]{1,0:T(8,128)(2,1)S(1)}, f32[1,128]{1,0:T(1,128)}, f32[16,1024]{1,0:T(8,128)}) custom-call(bf16[1024,1024]{1,0:T(8,128)(2,1)} %x_hbm.1, bf16[128,1024]{1,0:T(8,128)(2,1)} %win_hbm.1, bf16[128,1024]{1,0:T(8,128)(2,1)} %wout_hbm.1, bf16[4096,1024]{1,0:T(8,128)(2,1)} %k_hbm.1, s32[64,128]{1,0:T(8,128)} %bitcast.4, ...), custom_call_target="tpu_custom_call" | custom-call | tf_op jit(solution)/shard_map/queue_step/pallas_call | solution.py:495
  72.2 0.0 copy-start.1
  72.3 0.0 copy-start
  72.3 3.4 %copy.13 = bf16[4096,1024]{1,0:T(8,128)(2,1)} copy(bf16[4096,1024]{1,0:T(8,128)(2,1)S(1)} %get-tuple-element.9) | data formatting | bytes 16777216
  75.7 0.0 copy-done.1
  75.7 0.0 copy-done
  75.7 0.6 copy.15
Async XLA Ops:
  72.2 3.4 %copy-start.1 = (f32[1,128]{1,0:T(1,128)S(1)}, f32[1,128]{1,0:T(1,128)}, u32[]{:S(2)}) copy-start(f32[1,128]{1,0:T(1,128)} %get-tuple-element.7) | copy-start | bytes 1540
  72.3 3.5 %copy-start = (f32[16,1024]{1,0:T(8,128)S(1)}, f32[16,1024]{1,0:T(8,128)}, u32[]{:S(2)}) copy-start(f32[16,1024]{1,0:T(8,128)} %get-tuple-element.17) | copy-start | bytes 196612
